TPU v7x, 32 devices: a whole 2x2x4 slice. The times are simulated.
32 devices in a mesh: ctx: 8 (over z, x), head: 4 (over y, core).
Axes of the slice: x: 2, y: 2, z: 4, core: 2. Of those that a mesh axis runs over, the one named last changes fastest.
Arguments:
- keys: bfloat16 [16384, 5120], P('ctx', 'head'), may hold values from -6 to 6
- values: bfloat16 [16384, 5120], P('ctx', 'head'), may hold values from -6 to 6
- queries: bfloat16 [16384, 5120], P('ctx', 'head'), may hold values from -6 to 6
- rates: float32 [16384, 16], P('ctx', 'head'), may hold values from 9.765625e-05 to 0.0009765625
- w_gate: bfloat16 [320, 16, 320], P('ctx', 'head'), may hold values from -0.3125 to 0.3125
- w_up: bfloat16 [320, 16, 320], P('ctx', 'head'), may hold values from -0.3125 to 0.3125
- w_down: bfloat16 [320, 16, 320], P('ctx', 'head'), may hold values from -0.3125 to 0.3125
- gain: float32 [5120], P('head'), may hold values from 0.5 to 1.5
Outputs:
- output: bfloat16 [16384, 5120], P('ctx', 'head')
- new_gate: bfloat16 [320, 16, 320], P('ctx', 'head')
- new_up: bfloat16 [320, 16, 320], P('ctx', 'head')
- new_down: bfloat16 [320, 16, 320], P('ctx', 'head')
All inputs are finite; a program needn't handle non-finite values.
Results may differ from a plain program's by a relative error of at most 0.0092.
Values may be sent and summed in bfloat16 or wider, within the bound.
A program may use at most 128 MiB of HBM per device.

v0:
```python
import jax
import jax.numpy as jnp
from jax import lax
from jax.sharding import PartitionSpec as P

HEADS = 16
DH = 320
EPS = 1e-06


def per_device(keys, values, queries, rates, w_gate, w_up, w_down, gain):
    rows = keys.shape[0]
    heads = w_gate.shape[1]
    width = w_gate.shape[2]
    local_units = w_gate.shape[0]
    keyh = keys.reshape(rows, heads, width)
    valueh = values.reshape(rows, heads, width)
    queryh = queries.reshape(rows, heads, width)
    full_gate, full_up, full_down = (
        lax.all_gather(w_gate, "ctx", axis=0, tiled=True),
        lax.all_gather(w_up, "ctx", axis=0, tiled=True),
        lax.all_gather(w_down, "ctx", axis=0, tiled=True),
    )
    gpre = jnp.einsum("thd,fhd->thf", keyh, full_gate, preferred_element_type=jnp.float32)
    upre = jnp.einsum("thd,fhd->thf", keyh, full_up, preferred_element_type=jnp.float32)
    sig = jax.nn.sigmoid(gpre)
    act = gpre * sig
    slope = sig * (1.0 + gpre * (1.0 - sig))
    hidden = (act * upre).astype(jnp.bfloat16)
    scaled = (valueh.astype(jnp.float32) * rates[:, :, None]).astype(jnp.bfloat16)
    back = jnp.einsum("thd,fhd->thf", scaled, full_down, preferred_element_type=jnp.float32)
    dgate = (back * upre * slope).astype(jnp.bfloat16)
    dup = (back * act).astype(jnp.bfloat16)
    grad_gate = jnp.einsum("thf,thd->fhd", dgate, keyh, preferred_element_type=jnp.float32)
    grad_up = jnp.einsum("thf,thd->fhd", dup, keyh, preferred_element_type=jnp.float32)
    grad_down = jnp.einsum("thf,thd->fhd", hidden, scaled, preferred_element_type=jnp.float32)
    total = lax.psum(jnp.stack([grad_gate, grad_up, grad_down], axis=1), "ctx")
    olds = jnp.stack([full_gate, full_up, full_down], axis=1).astype(jnp.float32)
    updated = olds + total
    old_sq = jnp.sum(olds * olds, axis=0)
    new_sq = jnp.sum(updated * updated, axis=0)
    fresh = (updated * (jnp.sqrt(old_sq) * lax.rsqrt(new_sq + EPS))[None]).astype(jnp.bfloat16)
    offset = lax.axis_index("ctx") * local_units
    mine = lax.dynamic_slice_in_dim(fresh, offset, local_units, 0)
    new_gate = fresh[:, 0]
    new_up = fresh[:, 1]
    new_down = fresh[:, 2]
    qgate = jnp.einsum("thd,fhd->thf", queryh, new_gate, preferred_element_type=jnp.float32)
    qup = jnp.einsum("thd,fhd->thf", queryh, new_up, preferred_element_type=jnp.float32)
    mixed = (jax.nn.silu(qgate) * qup).astype(jnp.bfloat16)
    outh = jnp.einsum("thf,fhd->thd", mixed, new_down, preferred_element_type=jnp.float32)
    squares = lax.psum(jnp.sum(outh * outh, axis=(1, 2)), "head")
    scale = lax.rsqrt(squares / (HEADS * DH) + EPS)
    result = outh * scale[:, None, None] * gain.reshape(heads, width)[None]
    output = result.reshape(rows, heads * width).astype(jnp.bfloat16)
    return (output, mine[:, 0], mine[:, 1], mine[:, 2])


def solution(mesh):
    in_specs = (
        P("ctx", "head"),
        P("ctx", "head"),
        P("ctx", "head"),
        P("ctx", "head"),
        P("ctx", "head", None),
        P("ctx", "head", None),
        P("ctx", "head", None),
        P("head"),
    )
    out_specs = (
        P("ctx", "head"),
        P("ctx", "head", None),
        P("ctx", "head", None),
        P("ctx", "head", None),
    )
    return jax.shard_map(
        per_device, mesh=mesh, in_specs=in_specs, out_specs=out_specs, check_vma=False
    )
```

profile of v0, /device:TPU:0, one launch (start us, length us, event | category | flops | bytes accessed | tf_op | source)
XLA Modules:
  0.0 447.1 jit_solution(6353832946601583923)
XLA Ops:
  7.2 0.0 all-reduce.2.cloned.1.call-start
  7.2 7.9 %copy.31 = bf16[2048,1280]{0,1:T(8,128)(2,1)} copy(bf16[2048,1280]{1,0:T(8,128)(2,1)} %param.8) | data formatting | bytes 10485760 | tf_op args[0]
  15.2 34.4 %all_gather.9 = bf16[320,4,320]{2,0,1:T(8,128)(2,1)S(1)} all-gather(bf16[40,4,320]{2,0,1:T(8,128)(2,1)S(1)} %copy.27), channel_id=1, replica_groups=mesh['ctx'=8,'head'=4] {'ctx'}, dimensions={0}, use_global_device_ids=true | all-gather | bytes 921600 | tf_op jit(solution)/shard_map/all_gather | solution.py:20
  49.7 0.0 slice-start
  49.7 32.8 %all_gather.10 = bf16[320,4,320]{2,0,1:T(8,128)(2,1)S(1)} all-gather(bf16[40,4,320]{2,0,1:T(8,128)(2,1)S(1)} %copy.28), channel_id=1, replica_groups=mesh['ctx'=8,'head'=4] {'ctx'}, dimensions={0}, use_global_device_ids=true | all-gather | bytes 921600 | tf_op jit(solution)/shard_map/all_gather | solution.py:21
  82.4 8.1 %fusion.45 = f32[4,320,2048]{2,1,0:T(8,128)} fusion(bf16[320,4,320]{2,0,1:T(8,128)(2,1)S(1)} %all_gather.9, bf16[2048,4,320]{0,2,1:T(8,128)(2,1)} %bitcast.133), kind=kOutput, calls=%fused_computation.56 | convolution fusion | flops 1677721600 | bytes 16547840 | tf_op jit(solution)/shard_map/thd,fhd->thf/dot_general | solution.py:24
  90.5 5.4 %fusion.44 = f32[4,320,2048]{2,1,0:T(8,128)} fusion(bf16[320,4,320]{2,0,1:T(8,128)(2,1)S(1)} %all_gather.10, bf16[2048,4,320]{0,2,1:T(8,128)(2,1)S(1)} %bitcast.138), kind=kOutput, calls=%fused_computation.55 | convolution fusion | flops 1677721600 | bytes 16547840 | tf_op jit(solution)/shard_map/thd,fhd->thf/dot_general | solution.py:25
  95.9 8.0 %copy.30 = bf16[2048,1280]{0,1:T(8,128)(2,1)} copy(bf16[2048,1280]{1,0:T(8,128)(2,1)} %param.9) | data formatting | bytes 10485760 | tf_op args[1]
  103.9 33.2 %all_gather.11 = bf16[320,4,320]{2,0,1:T(8,128)(2,1)S(1)} all-gather(bf16[40,4,320]{2,0,1:T(8,128)(2,1)S(1)} %copy.29), channel_id=1, replica_groups=mesh['ctx'=8,'head'=4] {'ctx'}, dimensions={0}, use_global_device_ids=true | all-gather | bytes 921600 | tf_op jit(solution)/shard_map/all_gather | solution.py:22
  137.1 7.9 %fusion.24 = f32[4,2048,320]{1,2,0:T(8,128)} fusion(bf16[320,4,320]{2,0,1:T(8,128)(2,1)S(1)} %all_gather.11, bf16[2048,4,320]{0,2,1:T(8,128)(2,1)} %bitcast.143, f32[2048,4]{0,1:T(4,128)S(1)} %copy-done.4), kind=kOutput, calls=%fused_computation.36 | convolution fusion | flops 1685585920 | bytes 16580608 | tf_op jit(solution)/shard_map/thd,fhd->thf/dot_general | solution.py:31
  145.0 13.0 %fusion.31 = f32[320,1,4,320]{3,0,2,1:T(8,128)} fusion(f32[4,320,2048]{2,1,0:T(8,128)} %fusion.44, f32[4,320,2048]{2,1,0:T(8,128)} %fusion.45, bf16[2048,4,320]{0,2,1:T(8,128)(2,1)} %bitcast.144, f32[2048,4]{0,1:T(4,128)S(1)} %copy-done.4), kind=kOutput, calls=%fused_computation.40 | convolution fusion | flops 1701314560 | bytes 27885568 | tf_op jit(solution)/shard_map/thf,thd->fhd/dot_general | solution.py:36
  158.1 15.3 %fusion.28 = f32[320,1,4,320]{3,0,2,1:T(8,128)} fusion(bf16[2048,4,320]{0,2,1:T(8,128)(2,1)} %bitcast.134, f32[4,320,2048]{2,1,0:T(8,128)} %fusion.45, f32[4,320,2048]{2,1,0:T(8,128)} %fusion.44, f32[4,2048,320]{1,2,0:T(8,128)} %fusion.24), kind=kOutput, calls=%fused_computation.39 | convolution fusion | flops 1703936000 | bytes 38338560 | tf_op jit(solution)/shard_map/thf,thd->fhd/dot_general | solution.py:34
  173.3 10.7 %fusion.36 = f32[320,1,4,320]{3,0,2,1:T(8,128)S(1)} fusion(bf16[2048,4,320]{0,2,1:T(8,128)(2,1)} %bitcast.135, f32[4,2048,320]{1,2,0:T(8,128)} %fusion.24, f32[4,320,2048]{2,1,0:T(8,128)} %fusion.45), kind=kOutput, calls=%fused_computation.41 | convolution fusion | flops 1693450240 | bytes 27852800 | tf_op jit(solution)/shard_map/thf,thd->fhd/dot_general | solution.py:35
  184.1 3.0 pad_maximum_fusion
  187.1 0.0 all-reduce.2.cloned.1.call-update
  187.1 0.0 copy-start.8
  187.1 8.1 %copy.33 = bf16[2048,1280]{0,1:T(8,128)(2,1)} copy(bf16[2048,1280]{1,0:T(8,128)(2,1)} %param.10) | data formatting | bytes 10485760 | tf_op args[2]
  195.3 0.1 mul.103
  195.3 194.0 %all-reduce.2.cloned.1.call-done = f32[320,3,4,320]{3,0,2,1:T(8,128)} async-done(((f32[320,3,4,320]{3,0,2,1:T(8,128)}), f32[320,3,4,320]{3,0,2,1:T(8,128)}) %all-reduce.2.cloned.1.call-update) | async-done | bytes 4915216 | tf_op jit(solution)/shard_map/psum | solution.py:37
  389.4 3.6 fusion.14
  393.0 0.8 copy-done
  393.8 1.0 multiply_convert_fusion.1
  394.8 1.6 copy-done.1
  396.4 5.4 %fusion.39 = f32[4,320,2048]{2,1,0:T(8,128)} fusion(bf16[2048,4,320]{0,2,1:T(8,128)(2,1)S(1)} %bitcast.142, bf16[320,3,4,320]{3,0,2,1:T(8,128)(2,1)S(1)} %multiply_convert_fusion.1), kind=kOutput, calls=%fused_computation.44 | convolution fusion | flops 1677721600 | bytes 16711680 | tf_op jit(solution)/shard_map/thd,fhd->thf/dot_general | solution.py:48
  401.8 13.7 %multiply_reduce_fusion = (f32[2048]{0:T(1024)S(1)}, f32[4,320,2048]{2,1,0:T(8,128)}) fusion(f32[4,320,2048]{2,1,0:T(8,128)} %fusion.39, bf16[2048,4,320]{0,2,1:T(8,128)(2,1)} %bitcast.139, bf16[320,3,4,320]{3,0,2,1:T(8,128)(2,1)} %copy-done.1), kind=kOutput, calls=%fused_computation.25 | convolution fusion | flops 3376412672 | bytes 28188672 | tf_op jit(solution)/shard_map/thf,fhd->thd/dot_general | solution.py:51
  415.5 6.5 %psum.15 = f32[2048]{0:T(1024)S(1)} all-reduce(f32[2048]{0:T(1024)S(1)} %get-tuple-element.17), channel_id=1, replica_groups=mesh['ctx'=8,'head'=4] {'head'}, use_global_device_ids=true, to_apply=%region_4.5 | all-reduce | flops 2048 | bytes 16384 | tf_op jit(solution)/shard_map/psum | solution.py:52
  422.0 7.3 %multiply_convert_fusion = bf16[4,320,2048]{2,1,0:T(8,128)(2,1)} fusion(f32[4,320,2048]{2,1,0:T(8,128)} %get-tuple-element.18, f32[4,320]{1,0:T(4,128)S(1)} %mul.103, f32[2048]{0:T(1024)S(1)} %add_rsqrt_fusion), kind=kLoop, calls=%fused_computation.24 | loop fusion | flops 7864320 | bytes 15741952 | tf_op jit(solution)/shard_map/convert_element_type | solution.py:55
  429.3 7.9 %copy.35 = bf16[2048,1280]{1,0:T(8,128)(2,1)} copy(bf16[2048,1280]{0,1:T(8,128)(2,1)} %bitcast.145) | data formatting | bytes 10485760
  437.2 1.1 dynamic-slice_bitcast_fusion
  438.2 0.7 copy.36
  438.9 0.7 copy.37
  439.6 0.7 copy.38
  (29 shorter events, 0.1 us)
Async XLA Ops:
  7.2 8.0 %copy-start.5 = (bf16[40,4,320]{2,1,0:T(4,128)(2,1)S(1)}, bf16[40,4,320]{2,1,0:T(4,128)(2,1)}, u32[]{:S(2)}) copy-start(bf16[40,4,320]{2,1,0:T(4,128)(2,1)} %param.12) | copy-start | bytes 307204
  7.2 42.5 %copy-start.6 = (bf16[40,4,320]{2,1,0:T(4,128)(2,1)S(1)}, bf16[40,4,320]{2,1,0:T(4,128)(2,1)}, u32[]{:S(2)}) copy-start(bf16[40,4,320]{2,1,0:T(4,128)(2,1)} %param.13) | copy-start | bytes 307204
  7.2 382.2 %all-reduce.2.cloned.1.call-start = ((), (), s32[]{:S(2)}) async-start(), calls=%async_computation | async-start | bytes 11796480 | tf_op jit(solution)/shard_map/psum | solution.py:37
  49.7 40.9 %slice-start = ((s8[5242880]{0:T(1024)(128)(4,1)}), s8[4194304]{0:T(1024)(128)(4,1)S(1)}, s32[]{:S(2)}) async-start(s8[5242880]{0:T(1024)(128)(4,1)} %bitcast.136), calls=%async_computation.1 | async-start | bytes 8388608
  82.4 8.1 %slice-start.1 = ((s8[5242880]{0:T(1024)(128)(4,1)}), s8[1048576]{0:T(1024)(128)(4,1)S(1)}, s32[]{:S(2)}) async-start(s8[5242880]{0:T(1024)(128)(4,1)} %bitcast.136), calls=%async_computation.2 | async-start | bytes 2097152
  95.9 8.0 %copy-start.7 = (bf16[40,4,320]{2,1,0:T(4,128)(2,1)S(1)}, bf16[40,4,320]{2,1,0:T(4,128)(2,1)}, u32[]{:S(2)}) copy-start(bf16[40,4,320]{2,1,0:T(4,128)(2,1)} %param.14) | copy-start | bytes 307204
  95.9 41.2 %copy-start.4 = (f32[2048,4]{0,1:T(4,128)S(1)}, f32[2048,4]{0,1:T(4,128)}, u32[]{:S(2)}) copy-start(f32[2048,4]{0,1:T(4,128)} %param.11) | copy-start | bytes 98308
  173.3 10.7 %copy-start.2 = (f32[320,1,4,320]{3,0,2,1:T(8,128)S(1)}, f32[320,1,4,320]{3,0,2,1:T(8,128)}, u32[]{:S(2)}) copy-start(f32[320,1,4,320]{3,0,2,1:T(8,128)} %fusion.31) | copy-start | bytes 4915204
  173.3 10.7 %copy-start.3 = (f32[320,1,4,320]{3,0,2,1:T(8,128)S(1)}, f32[320,1,4,320]{3,0,2,1:T(8,128)}, u32[]{:S(2)}) copy-start(f32[320,1,4,320]{3,0,2,1:T(8,128)} %fusion.28) | copy-start | bytes 4915204
  187.1 8.2 %copy-start.8 = (f32[1280]{0:T(1024)S(1)}, f32[1280]{0:T(1024)}, u32[]{:S(2)}) copy-start(f32[1280]{0:T(1024)} %param.15) | copy-start | bytes 15364
  389.4 4.4 copy-start
  389.4 7.0 %slice-start.2 = ((s8[5242880]{0:T(1024)(128)(4,1)}), s8[4194304]{0:T(1024)(128)(4,1)S(1)}, s32[]{:S(2)}) async-start(s8[5242880]{0:T(1024)(128)(4,1)} %bitcast.140), calls=%async_computation.3 | async-start | bytes 8388608
  393.8 2.6 slice-start.3
  394.8 1.6 copy-start.1
Sparse Core Ops, SparseCore 0:
  187.2 202.0 all-reduce.1
where the time goes:
time: 448 us; the launch traced here: 447 us
  waiting for transfers between devices  194 us (43%)
  blocking collectives  107 us (24%)
  matrix products  79.5 us (18%)
  local copies, waits for them, and re-layouts  37.6 us (8%)
  other arithmetic  14.9 us (3%)
  between operations  14.2 us (3%)
    psum x1, waiting for transfers between devices, per_device(): total = lax.psum(jnp.stack([grad_gate, grad_up, grad_down], axis=1), 'ctx')  194 us
    unnamed x36, local copies, waits for them, and re-layouts  36.5 us
    all_gather x1, blocking collectives, per_device(): lax.all_gather(w_gate, 'ctx', axis=0, tiled=True)  34.4 us
    all_gather x1, blocking collectives, per_device(): lax.all_gather(w_down, 'ctx', axis=0, tiled=True)  33.2 us
    all_gather x1, blocking collectives, per_device(): lax.all_gather(w_up, 'ctx', axis=0, tiled=True)  32.8 us
    dot_general x1, matrix products, per_device(): jnp.einsum('thf,thd->fhd', dgate, keyh, preferred_element_type=jnp.float32)  15.3 us
    dot_general x1, matrix products, per_device(): jnp.einsum('thf,fhd->thd', mixed, new_down, preferred_element_type=jnp.fl...  13.7 us
    dot_general x1, matrix products, per_device(): jnp.einsum('thf,thd->fhd', hidden, scaled, preferred_element_type=jnp.flo...  13 us
  transfers between devices with their start and end apart: 1, of which 1 were waited for; matrix products, arithmetic and copies ran while one was open for 2% of the time, Pallas kernels for 0%

commit v1 on v0

--- a/solution.py
+++ b/solution.py
@@ -34,7 +34,9 @@
     grad_gate = jnp.einsum("thf,thd->fhd", dgate, keyh, preferred_element_type=jnp.float32)
     grad_up = jnp.einsum("thf,thd->fhd", dup, keyh, preferred_element_type=jnp.float32)
     grad_down = jnp.einsum("thf,thd->fhd", hidden, scaled, preferred_element_type=jnp.float32)
-    total = lax.psum(jnp.stack([grad_gate, grad_up, grad_down], axis=1), "ctx")
+    total = jnp.sum(
+        lax.all_gather(jnp.stack([grad_gate, grad_up, grad_down], axis=1), "ctx"), axis=0
+    )
     olds = jnp.stack([full_gate, full_up, full_down], axis=1).astype(jnp.float32)
     updated = olds + total
     old_sq = jnp.sum(olds * olds, axis=0)

time: 448 us -> 1160 us (2.59)
  waiting for transfers between devices: 194 us -> 886 us
  other arithmetic: 14.9 us -> 34.1 us
    all_gather x0 -> x1, waiting for transfers between devices: none -> 886 us  [per_device(): lax.all_gather(jnp.stack([grad_gate, grad_up, grad_down], axis=1), 'ctx')]
    psum x1 -> x0, waiting for transfers between devices: 194 us -> none  [per_device(): total = lax.psum(jnp.stack([grad_gate, grad_up, grad_down], axis=1), 'ctx')]
    reduce_sum x0 -> x1, other arithmetic: none -> 19.3 us  [per_device(): jnp.sum(lax.all_gather(jnp.stack([grad_gate, grad_up, grad_down], axis=1)...]
  transfers between devices with their start and end apart: 1 -> 1, of which waited for: 1 -> 1; matrix products, arithmetic and copies ran while one was open for 2% -> 1% of each run, Pallas kernels for 0% -> 0%
where the time goes in v1:
time: 1160 us
  waiting for transfers between devices  886 us (76%)
  blocking collectives  107 us (9%)
  matrix products  79.5 us (7%)
  local copies, waits for them, and re-layouts  37.4 us (3%)
  other arithmetic  34.1 us (3%)
  between operations  14.2 us (1%)
    all_gather x1, waiting for transfers between devices, per_device(): lax.all_gather(jnp.stack([grad_gate, grad_up, grad_down], axis=1), 'ctx')  886 us
    unnamed x36, local copies, waits for them, and re-layouts  36.2 us
    all_gather x1, blocking collectives, per_device(): lax.all_gather(w_gate, 'ctx', axis=0, tiled=True)  34.4 us
    all_gather x1, blocking collectives, per_device(): lax.all_gather(w_down, 'ctx', axis=0, tiled=True)  33 us
    all_gather x1, blocking collectives, per_device(): lax.all_gather(w_up, 'ctx', axis=0, tiled=True)  32.8 us
  transfers between devices with their start and end apart: 1, of which 1 were waited for; matrix products, arithmetic and copies ran while one was open for 1% of the time, Pallas kernels for 0%

profile of v1, /device:TPU:0, one launch (start us, length us, event | category | flops | bytes accessed | tf_op | source)
XLA Modules:
  0.0 1158.2 jit_solution(9646375408305158142)
XLA Ops:
  7.2 0.0 all-gather.3.cloned.1.call-start
  7.2 7.9 copy.31
  15.2 34.4 %all_gather.15 = bf16[320,4,320]{2,0,1:T(8,128)(2,1)S(1)} all-gather(bf16[40,4,320]{2,0,1:T(8,128)(2,1)S(1)} %copy.27), channel_id=1, replica_groups=mesh['ctx'=8,'head'=4] {'ctx'}, dimensions={0}, use_global_device_ids=true | all-gather | bytes 921600 | tf_op jit(solution)/shard_map/all_gather | solution.py:20
  49.7 0.0 slice-start
  49.7 32.8 %all_gather.16 = bf16[320,4,320]{2,0,1:T(8,128)(2,1)S(1)} all-gather(bf16[40,4,320]{2,0,1:T(8,128)(2,1)S(1)} %copy.28), channel_id=1, replica_groups=mesh['ctx'=8,'head'=4] {'ctx'}, dimensions={0}, use_global_device_ids=true | all-gather | bytes 921600 | tf_op jit(solution)/shard_map/all_gather | solution.py:21
  82.4 8.1 fusion.45
  90.5 5.4 fusion.44
  95.9 8.0 copy.30
  103.9 33.0 %all_gather.17 = bf16[320,4,320]{2,0,1:T(8,128)(2,1)S(1)} all-gather(bf16[40,4,320]{2,0,1:T(8,128)(2,1)S(1)} %copy.29), channel_id=1, replica_groups=mesh['ctx'=8,'head'=4] {'ctx'}, dimensions={0}, use_global_device_ids=true | all-gather | bytes 921600 | tf_op jit(solution)/shard_map/all_gather | solution.py:22
  136.9 7.9 fusion.24
  144.8 13.0 %fusion.31 = f32[320,1,4,320]{3,0,2,1:T(8,128)} fusion(f32[4,320,2048]{2,1,0:T(8,128)} %fusion.44, f32[4,320,2048]{2,1,0:T(8,128)} %fusion.45, bf16[2048,4,320]{0,2,1:T(8,128)(2,1)} %bitcast.146, f32[2048,4]{0,1:T(4,128)S(1)} %copy-done.4), kind=kOutput, calls=%fused_computation.40 | convolution fusion | flops 1701314560 | bytes 27885568 | tf_op jit(solution)/shard_map/thf,thd->fhd/dot_general | solution.py:36
  157.9 15.3 %fusion.28 = f32[320,1,4,320]{3,0,2,1:T(8,128)} fusion(bf16[2048,4,320]{0,2,1:T(8,128)(2,1)} %bitcast.135, f32[4,320,2048]{2,1,0:T(8,128)} %fusion.45, f32[4,320,2048]{2,1,0:T(8,128)} %fusion.44, f32[4,2048,320]{1,2,0:T(8,128)} %fusion.24), kind=kOutput, calls=%fused_computation.39 | convolution fusion | flops 1703936000 | bytes 38338560 | tf_op jit(solution)/shard_map/thf,thd->fhd/dot_general | solution.py:34
  173.2 10.7 fusion.36
  183.9 2.9 pad_maximum_fusion
  186.8 0.0 all-gather.3.cloned.1.call-update
  186.8 7.9 copy.33
  194.7 0.1 mul.103
  194.8 886.3 %all-gather.3.cloned.1.call-done = f32[2560,3,4,320]{3,0,2,1:T(8,128)} async-done(((f32[320,3,4,320]{3,0,2,1:T(8,128)}), f32[2560,3,4,320]{3,0,2,1:T(8,128)}) %all-gather.3.cloned.1.call-update) | async-done | bytes 39321616 | tf_op jit(solution)/shard_map/all_gather | solution.py:38
  1081.1 19.3 %reduce_sum.36 = f32[320,3,4,320]{3,0,2,1:T(8,128)} reduce(f32[8,320,3,4,320]{4,1,0,3,2:T(8,128)} %bitcast.140, f32[]{:T(128)} %constant.10.clone.1), dimensions={0}, to_apply=%region_0.0 | reduce | flops 8601600 | bytes 44236804 | tf_op jit(solution)/shard_map/reduce_sum | solution.py:37
  1100.4 3.6 fusion.14
  1104.0 0.8 copy-done
  1104.8 1.0 multiply_convert_fusion.1
  1105.9 1.6 copy-done.1
  1107.5 5.4 fusion.39
  1112.8 13.7 %multiply_reduce_fusion = (f32[2048]{0:T(1024)S(1)}, f32[4,320,2048]{2,1,0:T(8,128)}) fusion(f32[4,320,2048]{2,1,0:T(8,128)} %fusion.39, bf16[2048,4,320]{0,2,1:T(8,128)(2,1)} %bitcast.141, bf16[320,3,4,320]{3,0,2,1:T(8,128)(2,1)} %copy-done.1), kind=kOutput, calls=%fused_computation.25 | convolution fusion | flops 3376412672 | bytes 28188672 | tf_op jit(solution)/shard_map/thf,fhd->thd/dot_general | solution.py:53
  1126.6 6.5 psum.7
  1133.1 7.3 multiply_convert_fusion
  1140.3 7.9 copy.35
  1148.2 1.1 dynamic-slice_bitcast_fusion
  1149.3 0.7 copy.36
  1150.0 0.7 copy.37
  1150.6 0.7 copy.38
  (30 shorter events, 0.1 us)
Async XLA Ops:
  7.2 8.0 copy-start.5
  7.2 42.5 %copy-start.6 = (bf16[40,4,320]{2,1,0:T(4,128)(2,1)S(1)}, bf16[40,4,320]{2,1,0:T(4,128)(2,1)}, u32[]{:S(2)}) copy-start(bf16[40,4,320]{2,1,0:T(4,128)(2,1)} %param.13) | copy-start | bytes 307204
  7.2 1073.9 %all-gather.3.cloned.1.call-start = ((), (), s32[]{:S(2)}) async-start(), calls=%async_computation | async-start | bytes 53084160 | tf_op jit(solution)/shard_map/all_gather | solution.py:38
  49.7 40.9 %slice-start = ((s8[5242880]{0:T(1024)(128)(4,1)}), s8[4194304]{0:T(1024)(128)(4,1)S(1)}, s32[]{:S(2)}) async-start(s8[5242880]{0:T(1024)(128)(4,1)} %bitcast.137), calls=%async_computation.1 | async-start | bytes 8388608
  82.4 8.1 slice-start.1
  95.9 8.0 copy-start.7
  95.9 41.0 %copy-start.4 = (f32[2048,4]{0,1:T(4,128)S(1)}, f32[2048,4]{0,1:T(4,128)}, u32[]{:S(2)}) copy-start(f32[2048,4]{0,1:T(4,128)} %param.11) | copy-start | bytes 98308
  173.2 10.7 copy-start.2
  173.2 10.7 copy-start.3
  186.8 7.9 copy-start.8
  1100.4 4.4 copy-start
  1100.4 7.0 slice-start.2
  1104.8 2.6 slice-start.3
  1105.8 1.6 copy-start.1
Sparse Core Ops, SparseCore 0:
  186.9 894.0 all-gather.2
